TPU v7x, 32 devices: a whole 2x2x4 slice. The times are simulated.
32 devices in a mesh: loop: 4 (over y, core), inner: 8 (over z, x).
Axes of the slice: x: 2, y: 2, z: 4, core: 2. Of those that a mesh axis runs over, the one named last changes fastest.
Arguments:
- snapshots: bfloat16 [8192, 1024], P(('loop', 'inner')), may hold values from -6 to 6
- bins: int32 [8192], replicated, may hold values from 0 to 63, as said below
- pairs: int32 [256, 2], replicated, may hold values from 0 to 63, as said below
- start_weights: bfloat16 [1024, 32], replicated, may hold values from -0.1875 to 0.1875
Outputs:
- basis: float32 [8192, 96], P(('loop', 'inner'))
- coefficients: float32 [4, 32, 32], replicated
Inputs may be any that keep to these rules, and one draw needn't show every extreme that they name: `bins`: the snapshot in row n has a bin in [r * 8, (r + 1) * 8), where r = (n // 256) mod (8). `pairs`: every row (a, b) has a <= b <= a + 8; every bin is paired with itself.
All inputs are finite; a program needn't handle non-finite values.
Results may differ from a plain program's by a relative error of at most 0.0003.
Values may be sent and summed in bfloat16 or wider, within the bound.
No kernel may reach another device: no remote copies, remote signals or barrier semaphores. Data moves between devices by JAX's collectives and lax.ppermute only.
A program may use at most 64 MiB of HBM per device.

v0:
```python
import jax
import jax.numpy as jnp
from jax import lax
from jax.sharding import PartitionSpec as P

STEPS = 2
BINS_COL = 8


def extended(cells, sides, width):
    for axis, dim in sides:
        count = lax.axis_size(axis)
        ends = count - 1
        head = lax.slice_in_dim(cells, 0, width, axis=dim)
        tail = lax.slice_in_dim(cells, cells.shape[dim] - width, cells.shape[dim], axis=dim)
        cells = jnp.concatenate(
            [
                lax.ppermute(tail, axis, [(i, (i + 1) % count) for i in range(ends)]),
                cells,
                lax.ppermute(head, axis, [((i + 1) % count, i) for i in range(ends)]),
            ],
            axis=dim,
        )
    return cells


def matches(values, targets):
    return (values[:, None] == targets[None, :]).astype(jnp.float32)


def local_gram(left, right):
    return jnp.dot(left.T, right, precision=lax.Precision.HIGHEST)


def finish(matrix, gram_total):
    lower_factor = jnp.linalg.cholesky(gram_total)
    result = lax.linalg.triangular_solve(
        lower_factor, matrix, left_side=False, lower=True, transpose_a=True
    )
    return (result, lower_factor.T)


def local(snapshots, bins, pairs, start_weights):
    row_count, features = snapshots.shape
    block_width = start_weights.shape[1]
    n_loop = lax.axis_size("loop")
    n_inner = lax.axis_size("inner")
    column = lax.axis_index("inner")
    group = lax.axis_index("loop")
    bin_grid = jnp.pad(
        bins.reshape(n_loop, n_inner, row_count), ((0, 0), (1, 1), (0, 0)), constant_values=-1
    )
    side_rows = extended(snapshots, (("inner", 0),), row_count)
    partner_rows = lax.all_gather(side_rows[None], "loop", axis=0, tiled=True)
    tile_rows = partner_rows.reshape(n_loop * 3 * row_count, features)
    tile_bins = lax.dynamic_slice_in_dim(bin_grid, column, 3, 1).reshape(-1)
    my_bins = lax.dynamic_slice_in_dim(bins, (group * n_inner + column) * row_count, row_count)
    bin_base = column * BINS_COL
    my_ids = bin_base + jnp.arange(BINS_COL, dtype=jnp.int32)
    window_ids = bin_base - BINS_COL + jnp.arange(3 * BINS_COL, dtype=jnp.int32)
    left_bins = pairs[:, 0]
    right_bins = pairs[:, 1]
    pair_count = jnp.dot(
        matches(left_bins, my_ids).T,
        matches(right_bins, window_ids),
        precision=lax.Precision.HIGHEST,
    )
    pair_count = pair_count + jnp.dot(
        matches(right_bins, my_ids).T,
        matches(left_bins, window_ids),
        precision=lax.Precision.HIGHEST,
    )
    linked_bins = jnp.where(pair_count > 0.5, 1.0, 0.0).astype(jnp.float32)
    my_hot = matches(my_bins, my_ids)
    row_links = jnp.dot(my_hot, linked_bins)
    mine_wide = snapshots.astype(jnp.float32)
    mine_norms = jnp.sum(mine_wide * mine_wide, axis=1)
    epsilon = features / 3.0
    part_hot = matches(tile_bins, window_ids) * (tile_bins >= 0).astype(jnp.float32)[:, None]
    band_mask = jnp.dot(row_links, part_hot.T)
    part_wide = tile_rows.astype(jnp.float32)
    part_norms = jnp.sum(part_wide * part_wide, axis=1)
    products = lax.dot_general(
        snapshots, tile_rows, (((1,), (1,)), ((), ())), preferred_element_type=jnp.float32
    )
    distance = mine_norms[:, None] + part_norms[None, :] - 2.0 * products
    kept_tiles = [band_mask * jnp.exp(-distance / epsilon)]

    def current_kernel(which):
        return kept_tiles[which]

    degree = jnp.sum(current_kernel(0), axis=1)
    inv_root = lax.rsqrt(degree)
    start_block = jnp.dot(snapshots, start_weights, preferred_element_type=jnp.float32)
    start_total = lax.psum(local_gram(start_block, start_block), ("loop", "inner"))
    current, unused = finish(start_block, start_total)
    basis_blocks = [current]
    coefficients = []
    previous = current
    prev_b = jnp.zeros((block_width, block_width), jnp.float32)
    for lanczos_step in range(STEPS):
        scaled = inv_root[:, None] * current
        vec_side = extended(scaled, (("inner", 0),), row_count)
        vec_strip = lax.all_gather(vec_side[None], "loop", axis=0, tiled=True)
        strip = vec_strip.reshape(n_loop * 3 * row_count, block_width)
        total = jnp.dot(current_kernel(0), strip, precision=lax.Precision.HIGHEST)
        image = inv_root[:, None] * total
        projected = lax.psum(local_gram(current, image), ("loop", "inner"))
        image = image - jnp.dot(current, projected, precision=lax.Precision.HIGHEST)
        if lanczos_step > 0:
            image = image - jnp.dot(previous, prev_b.T, precision=lax.Precision.HIGHEST)
        gram_total = lax.psum(local_gram(image, image), ("loop", "inner"))
        following, factor = finish(image, gram_total)
        coefficients.append(projected)
        coefficients.append(factor)
        previous = current
        prev_b = factor
        current = following
        basis_blocks.append(current)
    return (jnp.concatenate(basis_blocks, axis=1), jnp.stack(coefficients))


def solution(mesh):
    in_specs = (P(("loop", "inner"), None), P(), P(), P())
    out_specs = (P(("loop", "inner"), None), P())
    return jax.shard_map(local, mesh=mesh, in_specs=in_specs, out_specs=out_specs, check_vma=False)
```

profile of v0, /device:TPU:0, one launch (start us, length us, event | category | flops | bytes accessed | tf_op | source)
XLA Modules:
  0.0 321.3 jit_solution(17234646396150438926)
XLA Ops:
  7.2 0.0 copy-start
  7.2 0.0 copy-start.2
  7.2 0.0 all-gather.5.cloned.1.call-start
  7.3 1.4 collective-permute-start.1
  8.7 5.5 %collective-permute-start = (bf16[256,1024]{1,0:T(8,128)(2,1)}, bf16[256,1024]{1,0:T(8,128)(2,1)S(1)}, u32[]{:S(2)}, u32[]{:S(2)}) collective-permute-start(bf16[256,1024]{1,0:T(8,128)(2,1)} %param.7), channel_id=1, source_target_pairs={{0,1},{1,2},{2,3},{3,4},{4,5},{5,6},{6,7},{8,9},{9,10},{10,11},{11... | collective-permute-start | bytes 1572872 | tf_op jit(solution)/shard_map/ppermute | solution.py:18
  14.2 10.2 %collective-permute-done.1 = bf16[256,1024]{1,0:T(8,128)(2,1)S(1)} collective-permute-done((bf16[256,1024]{1,0:T(8,128)(2,1)}, bf16[256,1024]{1,0:T(8,128)(2,1)S(1)}, u32[]{:S(2)}, u32[]{:S(2)}) %collective-permute-start.1) | collective-permute-done | bytes 524320 | tf_op jit(solution)/shard_map/ppermute | solution.py:20
  24.4 11.5 %collective-permute-done = bf16[256,1024]{1,0:T(8,128)(2,1)S(1)} collective-permute-done((bf16[256,1024]{1,0:T(8,128)(2,1)}, bf16[256,1024]{1,0:T(8,128)(2,1)S(1)}, u32[]{:S(2)}, u32[]{:S(2)}) %collective-permute-start) | collective-permute-done | bytes 524320 | tf_op jit(solution)/shard_map/ppermute | solution.py:18
  35.9 2.3 pad_maximum_fusion
  38.2 0.0 all-gather.5.cloned.1.call-update
  38.3 0.1 dynamic_slice.6
  38.4 0.2 fusion.55
  38.6 0.2 fusion.56
  38.8 42.3 %psum.35 = f32[32,32]{0,1:T(8,128)S(1)} all-reduce(f32[32,32]{0,1:T(8,128)S(1)} %fusion.56), channel_id=1, replica_groups=mesh['loop'=4,'inner'=8] {'loop','inner'}, use_global_device_ids=true, to_apply=%region_0.1 | all-reduce | flops 1024 | bytes 8192 | tf_op jit(solution)/shard_map/psum | solution.py:95
  81.1 0.1 copy.27
  81.2 2.9 cholesky.59
  84.1 0.6 compare_reduce_fusion.2
  84.8 0.7 fusion.35
  85.4 2.4 custom-call.7
  87.9 0.2 multiply_reduce_fusion.1
  88.1 0.3 fusion.20
  88.4 0.3 fusion.9
  88.6 0.0 all-gather.5.cloned.1.call-done
  88.7 4.2 %multiply_reduce_fusion = f32[3072]{0:T(1024)S(1)} fusion(bf16[3072,1024]{1,0:T(8,128)(2,1)} %all-gather.5.cloned.1.call-done), kind=kLoop, calls=%fused_computation | loop fusion | flops 9434112 | bytes 6303744 | tf_op jit(solution)/shard_map/reduce_sum | solution.py:82
  92.9 0.4 copy-done.1
  93.3 4.0 %fusion.4 = f32[256,3072]{1,0:T(8,128)} fusion(bf16[3072,1024]{1,0:T(8,128)(2,1)S(1)} %copy-done.1, bf16[256,1024]{1,0:T(8,128)(2,1)S(1)} %copy-done.2, f32[3072]{0:T(1024)S(1)} %multiply_reduce_fusion, f32[256]{0:T(256)S(1)} %multiply_reduce_fusion.1), kind=kOutput, calls=%fused_computation.7 | convolution fusion | flops 1614544896 | bytes 9974784 | tf_op jit(solution)/shard_map/dot_general | solution.py:83
  97.3 2.8 fusion.52
  100.1 0.2 broadcast_multiply_fusion.1
  100.3 1.3 collective-permute-start.3
  101.6 4.8 %collective-permute-start.2 = (f32[256,32]{0,1:T(8,128)S(1)}, f32[256,32]{0,1:T(8,128)S(1)}, u32[]{:S(2)}, u32[]{:S(2)}) collective-permute-start(f32[256,32]{0,1:T(8,128)S(1)} %get-tuple-element.18), channel_id=1, source_target_pairs={{0,1},{1,2},{2,3},{3,4},{4,5},{5,6},{6,7},{8,9},{9,10},{10,11},{11... | collective-permute-start | bytes 98312 | tf_op jit(solution)/shard_map/ppermute | solution.py:18
  106.4 0.0 collective-permute-done.3
  106.4 1.6 collective-permute-done.2
  108.0 7.2 %all-gather.1 = f32[3072,32]{0,1:T(8,128)S(1)} all-gather(f32[768,32]{0,1:T(8,128)S(1)} %pad_maximum_fusion.1), channel_id=3, replica_groups=mesh['loop'=4,'inner'=8] {'loop'}, dimensions={0}, use_global_device_ids=true | all-gather | bytes 491520 | tf_op jit(solution)/shard_map/all_gather | solution.py:104
  115.2 2.8 convolution_multiply_fusion.3
  118.0 0.2 fusion.57
  118.1 41.4 %psum.36 = f32[32,32]{0,1:T(8,128)S(1)} all-reduce(f32[32,32]{0,1:T(8,128)S(1)} %fusion.57), channel_id=1, replica_groups=mesh['loop'=4,'inner'=8] {'loop','inner'}, use_global_device_ids=true, to_apply=%region_6.9 | all-reduce | flops 1024 | bytes 8192 | tf_op jit(solution)/shard_map/psum | solution.py:108
  159.5 0.2 convolution_subtract_fusion.1
  159.7 0.2 fusion.58
  159.9 39.5 %psum.37 = f32[32,32]{0,1:T(8,128)S(1)} all-reduce(f32[32,32]{0,1:T(8,128)S(1)} %fusion.58), channel_id=1, replica_groups=mesh['loop'=4,'inner'=8] {'loop','inner'}, use_global_device_ids=true, to_apply=%region_7.10 | all-reduce | flops 1024 | bytes 8192 | tf_op jit(solution)/shard_map/psum | solution.py:112
  199.4 0.1 copy.31
  199.4 2.9 cholesky.70
  202.4 0.6 compare_reduce_fusion.1
  203.0 0.7 fusion.43
  203.7 2.4 custom-call.8
  206.1 0.2 broadcast_multiply_fusion
  206.4 1.3 collective-permute-start.5
  207.7 4.8 %collective-permute-start.4 = (f32[256,32]{0,1:T(8,128)S(1)}, f32[256,32]{0,1:T(8,128)S(1)}, u32[]{:S(2)}, u32[]{:S(2)}) collective-permute-start(f32[256,32]{0,1:T(8,128)S(1)} %get-tuple-element.20), channel_id=1, source_target_pairs={{0,1},{1,2},{2,3},{3,4},{4,5},{5,6},{6,7},{8,9},{9,10},{10,11},{11... | collective-permute-start | bytes 98312 | tf_op jit(solution)/shard_map/ppermute | solution.py:18
  212.5 0.9 fusion.44
  213.4 0.0 collective-permute-done.5
  213.4 0.7 collective-permute-done.4
  214.1 7.2 %all-gather.2 = f32[3072,32]{0,1:T(8,128)S(1)} all-gather(f32[768,32]{0,1:T(8,128)S(1)} %pad_maximum_fusion.2), channel_id=4, replica_groups=mesh['loop'=4,'inner'=8] {'loop'}, dimensions={0}, use_global_device_ids=true | all-gather | bytes 491520 | tf_op jit(solution)/shard_map/all_gather | solution.py:104
  221.3 2.8 convolution_multiply_fusion.2
  224.0 0.2 fusion.59
  224.2 41.7 %psum.38 = f32[32,32]{0,1:T(8,128)S(1)} all-reduce(f32[32,32]{0,1:T(8,128)S(1)} %fusion.59), channel_id=1, replica_groups=mesh['loop'=4,'inner'=8] {'loop','inner'}, use_global_device_ids=true, to_apply=%region_8.11 | all-reduce | flops 1024 | bytes 8192 | tf_op jit(solution)/shard_map/psum | solution.py:108
  265.9 0.2 fusion.5
  266.1 0.2 fusion.60
  266.3 39.8 %psum.39 = f32[32,32]{0,1:T(8,128)S(1)} all-reduce(f32[32,32]{0,1:T(8,128)S(1)} %fusion.60), channel_id=1, replica_groups=mesh['loop'=4,'inner'=8] {'loop','inner'}, use_global_device_ids=true, to_apply=%region_9.12 | all-reduce | flops 1024 | bytes 8192 | tf_op jit(solution)/shard_map/psum | solution.py:112
  306.1 0.1 copy.34
  306.2 2.9 cholesky.81
  309.1 0.6 compare_reduce_fusion
  309.8 0.7 fusion.42
  310.4 2.4 custom-call.9
  312.9 0.2 convolution_bitcast_fusion
  313.1 0.6 pad_maximum_fusion.3
  313.8 0.7 copy.35
  (24 shorter events, 0.2 us)
Async XLA Ops:
  7.2 31.2 %copy-start = (bf16[1024,32]{0,1:T(8,128)(2,1)S(1)}, bf16[1024,32]{0,1:T(8,128)(2,1)}, u32[]{:S(2)}) copy-start(bf16[1024,32]{0,1:T(8,128)(2,1)} %param.10) | copy-start | bytes 196612
  7.2 31.2 %copy-start.2 = (bf16[256,1024]{1,0:T(8,128)(2,1)S(1)}, bf16[256,1024]{1,0:T(8,128)(2,1)}, u32[]{:S(2)}) copy-start(bf16[256,1024]{1,0:T(8,128)(2,1)} %param.7) | copy-start | bytes 1572868
  7.2 31.0 %copy-start.3 = (s32[8192]{0:T(1024)S(1)}, s32[8192]{0:T(1024)}, u32[]{:S(2)}) copy-start(s32[8192]{0:T(1024)} %param.8) | copy-start | bytes 98308
  7.2 80.9 %copy-start.4 = (s32[256,2]{0,1:T(2,128)S(1)}, s32[256,2]{0,1:T(2,128)}, u32[]{:S(2)}) copy-start(s32[256,2]{0,1:T(2,128)} %param.9) | copy-start | bytes 6148
  7.2 81.4 %all-gather.5.cloned.1.call-start = ((), (), s32[]{:S(2)}) async-start(), calls=%async_computation | async-start | bytes 7864320 | tf_op jit(solution)/shard_map/all_gather | solution.py:54
  7.3 17.1 %collective-permute-start.1 = (bf16[256,1024]{1,0:T(8,128)(2,1)}, bf16[256,1024]{1,0:T(8,128)(2,1)S(1)}, u32[]{:S(2)}, u32[]{:S(2)}) collective-permute-start(bf16[256,1024]{1,0:T(8,128)(2,1)} %param.7), channel_id=1, source_target_pairs={{1,0},{2,1},{3,2},{4,3},{5,4},{6,5},{7,6},{9,8},{10,9},{11,10},{12... | collective-permute-start | bytes 1572872 | tf_op jit(solution)/shard_map/ppermute | solution.py:20
  8.7 27.2 %collective-permute-start = (bf16[256,1024]{1,0:T(8,128)(2,1)}, bf16[256,1024]{1,0:T(8,128)(2,1)S(1)}, u32[]{:S(2)}, u32[]{:S(2)}) collective-permute-start(bf16[256,1024]{1,0:T(8,128)(2,1)} %param.7), channel_id=1, source_target_pairs={{0,1},{1,2},{2,3},{3,4},{4,5},{5,6},{6,7},{8,9},{9,10},{10,11},{11... | collective-permute-start | bytes 1572872 | tf_op jit(solution)/shard_map/ppermute | solution.py:18
  88.7 4.6 %copy-start.1 = (bf16[3072,1024]{1,0:T(8,128)(2,1)S(1)}, bf16[3072,1024]{1,0:T(8,128)(2,1)}, u32[]{:S(2)}) copy-start(bf16[3072,1024]{1,0:T(8,128)(2,1)} %all-gather.5.cloned.1.call-done) | copy-start | bytes 18874372
  100.3 6.1 %collective-permute-start.3 = (f32[256,32]{0,1:T(8,128)S(1)}, f32[256,32]{0,1:T(8,128)S(1)}, u32[]{:S(2)}, u32[]{:S(2)}) collective-permute-start(f32[256,32]{0,1:T(8,128)S(1)} %get-tuple-element.18), channel_id=1, source_target_pairs={{1,0},{2,1},{3,2},{4,3},{5,4},{6,5},{7,6},{9,8},{10,9},{11,10},{12... | collective-permute-start | bytes 98312 | tf_op jit(solution)/shard_map/ppermute | solution.py:20
  101.6 6.4 %collective-permute-start.2 = (f32[256,32]{0,1:T(8,128)S(1)}, f32[256,32]{0,1:T(8,128)S(1)}, u32[]{:S(2)}, u32[]{:S(2)}) collective-permute-start(f32[256,32]{0,1:T(8,128)S(1)} %get-tuple-element.18), channel_id=1, source_target_pairs={{0,1},{1,2},{2,3},{3,4},{4,5},{5,6},{6,7},{8,9},{9,10},{10,11},{11... | collective-permute-start | bytes 98312 | tf_op jit(solution)/shard_map/ppermute | solution.py:18
  206.4 7.0 %collective-permute-start.5 = (f32[256,32]{0,1:T(8,128)S(1)}, f32[256,32]{0,1:T(8,128)S(1)}, u32[]{:S(2)}, u32[]{:S(2)}) collective-permute-start(f32[256,32]{0,1:T(8,128)S(1)} %get-tuple-element.20), channel_id=1, source_target_pairs={{1,0},{2,1},{3,2},{4,3},{5,4},{6,5},{7,6},{9,8},{10,9},{11,10},{12... | collective-permute-start | bytes 98312 | tf_op jit(solution)/shard_map/ppermute | solution.py:20
  207.7 6.4 %collective-permute-start.4 = (f32[256,32]{0,1:T(8,128)S(1)}, f32[256,32]{0,1:T(8,128)S(1)}, u32[]{:S(2)}, u32[]{:S(2)}) collective-permute-start(f32[256,32]{0,1:T(8,128)S(1)} %get-tuple-element.20), channel_id=1, source_target_pairs={{0,1},{1,2},{2,3},{3,4},{4,5},{5,6},{6,7},{8,9},{9,10},{10,11},{11... | collective-permute-start | bytes 98312 | tf_op jit(solution)/shard_map/ppermute | solution.py:18
Sparse Core Ops, SparseCore 0:
  38.3 48.3 all-gather.4
where the time goes:
time: 323 us; the launch traced here: 321 us
  blocking collectives  219 us (68%)
  other arithmetic  27.5 us (9%)
  waiting for transfers between devices  24 us (7%)
  starting transfers between devices  19.2 us (6%)
  matrix products  15.9 us (5%)
  between operations  14.4 us (4%)
    psum x2, blocking collectives, local(): projected = lax.psum(local_gram(current, image), ('loop', 'inner'))  83.1 us
    psum x2, blocking collectives, local(): gram_total = lax.psum(local_gram(image, image), ('loop', 'inner'))  79.3 us
    psum x1, blocking collectives, local(): lax.psum(local_gram(start_block, start_block), ('loop', 'inner'))  42.3 us
    ppermute x3, starting transfers between devices, extended(): lax.ppermute(tail, axis, [(i, (i + 1) % count) for i in range(ends)])  15.1 us
    all_gather x2, blocking collectives, local(): vec_strip = lax.all_gather(vec_side[None], 'loop', axis=0, tiled=True)  14.3 us
    ppermute x3, waiting for transfers between devices, extended(): lax.ppermute(tail, axis, [(i, (i + 1) % count) for i in range(ends)])  13.8 us
    another operation x9, other arithmetic, finish(): lower_factor = jnp.linalg.cholesky(gram_total)  10.8 us
    ppermute x3, waiting for transfers between devices, extended(): lax.ppermute(head, axis, [((i + 1) % count, i) for i in range(ends)])  10.2 us
  transfers between devices with their start and end apart: 7, of which 4 were waited for; matrix products, arithmetic and copies ran while one was open for 3% of the time, Pallas kernels for 0%

commit v1 on v0

--- a/solution.py
+++ b/solution.py
@@ -109,7 +109,7 @@
         image = image - jnp.dot(current, projected, precision=lax.Precision.HIGHEST)
         if lanczos_step > 0:
             image = image - jnp.dot(previous, prev_b.T, precision=lax.Precision.HIGHEST)
-        gram_total = lax.psum(local_gram(image, image), ("loop", "inner"))
+        gram_total = lax.psum(lax.psum(local_gram(image, image), "inner"), "loop")
         following, factor = finish(image, gram_total)
         coefficients.append(projected)
         coefficients.append(factor)

time: 323 us -> 332 us (1.028)
  blocking collectives: 219 us -> 229 us
    psum x2 -> x4, blocking collectives: 79.3 us -> 92.4 us  [local(): gram_total = lax.psum(lax.psum(local_gram(image, image), 'inner'), 'loop')]
where the time goes in v1:
time: 332 us; the launch traced here: 331 us
  blocking collectives  229 us (69%)
  other arithmetic  27.5 us (8%)
  waiting for transfers between devices  23.9 us (7%)
  starting transfers between devices  18.9 us (6%)
  matrix products  15.9 us (5%)
  between operations  14.4 us (4%)
    psum x4, blocking collectives, local(): gram_total = lax.psum(lax.psum(local_gram(image, image), 'inner'), 'loop')  92.4 us
    psum x2, blocking collectives, local(): projected = lax.psum(local_gram(current, image), ('loop', 'inner'))  80.9 us
    psum x1, blocking collectives, local(): lax.psum(local_gram(start_block, start_block), ('loop', 'inner'))  42.3 us
    ppermute x3, starting transfers between devices, extended(): lax.ppermute(tail, axis, [(i, (i + 1) % count) for i in range(ends)])  14.9 us
    ppermute x3, waiting for transfers between devices, extended(): lax.ppermute(tail, axis, [(i, (i + 1) % count) for i in range(ends)])  13.8 us
    all_gather x2, blocking collectives, local(): vec_strip = lax.all_gather(vec_side[None], 'loop', axis=0, tiled=True)  13.5 us
    another operation x9, other arithmetic, finish(): lower_factor = jnp.linalg.cholesky(gram_total)  10.8 us
    ppermute x3, waiting for transfers between devices, extended(): lax.ppermute(head, axis, [((i + 1) % count, i) for i in range(ends)])  10.2 us
  transfers between devices with their start and end apart: 7, of which 4 were waited for; matrix products, arithmetic and copies ran while one was open for 3% of the time, Pallas kernels for 0%

profile of v1, /device:TPU:0, one launch (start us, length us, event | category | flops | bytes accessed | tf_op | source)
XLA Modules:
  0.0 331.2 jit_solution(6104345148274427128)
XLA Ops:
  7.2 0.0 copy-start
  7.2 0.0 all-gather.5.cloned.1.call-start
  7.3 1.4 collective-permute-start.1
  8.7 5.5 %collective-permute-start = (bf16[256,1024]{1,0:T(8,128)(2,1)}, bf16[256,1024]{1,0:T(8,128)(2,1)S(1)}, u32[]{:S(2)}, u32[]{:S(2)}) collective-permute-start(bf16[256,1024]{1,0:T(8,128)(2,1)} %param.7), channel_id=1, source_target_pairs={{0,1},{1,2},{2,3},{3,4},{4,5},{5,6},{6,7},{8,9},{9,10},{10,11},{11... | collective-permute-start | bytes 1572872 | tf_op jit(solution)/shard_map/ppermute | solution.py:18
  14.2 10.2 %collective-permute-done.1 = bf16[256,1024]{1,0:T(8,128)(2,1)S(1)} collective-permute-done((bf16[256,1024]{1,0:T(8,128)(2,1)}, bf16[256,1024]{1,0:T(8,128)(2,1)S(1)}, u32[]{:S(2)}, u32[]{:S(2)}) %collective-permute-start.1) | collective-permute-done | bytes 524320 | tf_op jit(solution)/shard_map/ppermute | solution.py:20
  24.4 11.5 %collective-permute-done = bf16[256,1024]{1,0:T(8,128)(2,1)S(1)} collective-permute-done((bf16[256,1024]{1,0:T(8,128)(2,1)}, bf16[256,1024]{1,0:T(8,128)(2,1)S(1)}, u32[]{:S(2)}, u32[]{:S(2)}) %collective-permute-start) | collective-permute-done | bytes 524320 | tf_op jit(solution)/shard_map/ppermute | solution.py:18
  35.9 2.3 pad_maximum_fusion
  38.2 0.0 all-gather.5.cloned.1.call-update
  38.3 0.1 dynamic_slice.6
  38.4 0.2 fusion.55
  38.6 0.2 fusion.56
  38.8 42.3 %psum.49 = f32[32,32]{0,1:T(8,128)S(1)} all-reduce(f32[32,32]{0,1:T(8,128)S(1)} %fusion.56), channel_id=1, replica_groups=mesh['loop'=4,'inner'=8] {'loop','inner'}, use_global_device_ids=true, to_apply=%region_0.1 | all-reduce | flops 1024 | bytes 8192 | tf_op jit(solution)/shard_map/psum | solution.py:95
  81.1 0.1 copy.27
  81.2 2.9 cholesky.59
  84.1 0.6 compare_reduce_fusion.2
  84.8 0.7 fusion.35
  85.4 2.4 custom-call.7
  87.9 0.2 multiply_reduce_fusion.1
  88.1 0.3 fusion.20
  88.4 0.3 fusion.9
  88.6 0.0 all-gather.5.cloned.1.call-done
  88.7 4.2 %multiply_reduce_fusion = f32[3072]{0:T(1024)S(1)} fusion(bf16[3072,1024]{1,0:T(8,128)(2,1)} %all-gather.5.cloned.1.call-done), kind=kLoop, calls=%fused_computation | loop fusion | flops 9434112 | bytes 6303744 | tf_op jit(solution)/shard_map/reduce_sum | solution.py:82
  92.9 0.4 copy-done.1
  93.3 4.0 %fusion.4 = f32[256,3072]{1,0:T(8,128)} fusion(bf16[3072,1024]{1,0:T(8,128)(2,1)S(1)} %copy-done.1, bf16[256,1024]{1,0:T(8,128)(2,1)S(1)} %copy-done.2, f32[3072]{0:T(1024)S(1)} %multiply_reduce_fusion, f32[256]{0:T(256)S(1)} %multiply_reduce_fusion.1), kind=kOutput, calls=%fused_computation.7 | convolution fusion | flops 1614544896 | bytes 9974784 | tf_op jit(solution)/shard_map/dot_general | solution.py:83
  97.3 2.8 fusion.52
  100.1 0.2 broadcast_multiply_fusion.1
  100.3 1.3 collective-permute-start.3
  101.6 4.8 %collective-permute-start.2 = (f32[256,32]{0,1:T(8,128)S(1)}, f32[256,32]{0,1:T(8,128)S(1)}, u32[]{:S(2)}, u32[]{:S(2)}) collective-permute-start(f32[256,32]{0,1:T(8,128)S(1)} %get-tuple-element.18), channel_id=1, source_target_pairs={{0,1},{1,2},{2,3},{3,4},{4,5},{5,6},{6,7},{8,9},{9,10},{10,11},{11... | collective-permute-start | bytes 98312 | tf_op jit(solution)/shard_map/ppermute | solution.py:18
  106.4 0.0 collective-permute-done.3
  106.4 1.6 collective-permute-done.2
  108.0 7.2 %all-gather.1 = f32[3072,32]{0,1:T(8,128)S(1)} all-gather(f32[768,32]{0,1:T(8,128)S(1)} %pad_maximum_fusion.1), channel_id=3, replica_groups=mesh['loop'=4,'inner'=8] {'loop'}, dimensions={0}, use_global_device_ids=true | all-gather | bytes 491520 | tf_op jit(solution)/shard_map/all_gather | solution.py:104
  115.2 2.8 convolution_multiply_fusion.3
  118.0 0.2 fusion.57
  118.1 41.4 %psum.50 = f32[32,32]{0,1:T(8,128)S(1)} all-reduce(f32[32,32]{0,1:T(8,128)S(1)} %fusion.57), channel_id=1, replica_groups=mesh['loop'=4,'inner'=8] {'loop','inner'}, use_global_device_ids=true, to_apply=%region_6.9 | all-reduce | flops 1024 | bytes 8192 | tf_op jit(solution)/shard_map/psum | solution.py:108
  159.5 0.2 convolution_subtract_fusion.1
  159.7 0.2 fusion.58
  159.9 36.1 %psum.51 = f32[32,32]{0,1:T(8,128)S(1)} all-reduce(f32[32,32]{0,1:T(8,128)S(1)} %fusion.58), channel_id=1, replica_groups=mesh['loop'=4,'inner'=8] {'inner'}, use_global_device_ids=true, to_apply=%region_7.10 | all-reduce | flops 1024 | bytes 8192 | tf_op jit(solution)/shard_map/psum | solution.py:112
  196.0 10.1 %psum.52 = f32[32,32]{0,1:T(8,128)S(1)} all-reduce(f32[32,32]{0,1:T(8,128)S(1)} %psum.51), channel_id=1, replica_groups=mesh['loop'=4,'inner'=8] {'loop'}, use_global_device_ids=true, to_apply=%region_8.11 | all-reduce | flops 1024 | bytes 8192 | tf_op jit(solution)/shard_map/psum | solution.py:112
  206.1 0.1 copy.31
  206.2 2.9 cholesky.70
  209.1 0.6 compare_reduce_fusion.1
  209.8 0.7 fusion.43
  210.4 2.4 custom-call.8
  212.9 0.2 broadcast_multiply_fusion
  213.1 1.3 collective-permute-start.5
  214.4 4.5 %collective-permute-start.4 = (f32[256,32]{0,1:T(8,128)S(1)}, f32[256,32]{0,1:T(8,128)S(1)}, u32[]{:S(2)}, u32[]{:S(2)}) collective-permute-start(f32[256,32]{0,1:T(8,128)S(1)} %get-tuple-element.20), channel_id=1, source_target_pairs={{0,1},{1,2},{2,3},{3,4},{4,5},{5,6},{6,7},{8,9},{9,10},{10,11},{11... | collective-permute-start | bytes 98312 | tf_op jit(solution)/shard_map/ppermute | solution.py:18
  219.0 0.9 fusion.44
  219.9 0.7 collective-permute-done.4
  220.6 6.3 %all-gather.2 = f32[3072,32]{0,1:T(8,128)S(1)} all-gather(f32[768,32]{0,1:T(8,128)S(1)} %pad_maximum_fusion.2), channel_id=4, replica_groups=mesh['loop'=4,'inner'=8] {'loop'}, dimensions={0}, use_global_device_ids=true | all-gather | bytes 491520 | tf_op jit(solution)/shard_map/all_gather | solution.py:104
  226.9 2.8 convolution_multiply_fusion.2
  229.7 0.2 fusion.59
  229.8 39.5 %psum.53 = f32[32,32]{0,1:T(8,128)S(1)} all-reduce(f32[32,32]{0,1:T(8,128)S(1)} %fusion.59), channel_id=1, replica_groups=mesh['loop'=4,'inner'=8] {'loop','inner'}, use_global_device_ids=true, to_apply=%region_9.12 | all-reduce | flops 1024 | bytes 8192 | tf_op jit(solution)/shard_map/psum | solution.py:108
  269.4 0.2 fusion.5
  269.5 0.2 fusion.60
  269.7 36.1 %psum.54 = f32[32,32]{0,1:T(8,128)S(1)} all-reduce(f32[32,32]{0,1:T(8,128)S(1)} %fusion.60), channel_id=1, replica_groups=mesh['loop'=4,'inner'=8] {'inner'}, use_global_device_ids=true, to_apply=%region_10.13 | all-reduce | flops 1024 | bytes 8192 | tf_op jit(solution)/shard_map/psum | solution.py:112
  305.8 10.1 %psum.55 = f32[32,32]{0,1:T(8,128)S(1)} all-reduce(f32[32,32]{0,1:T(8,128)S(1)} %psum.54), channel_id=1, replica_groups=mesh['loop'=4,'inner'=8] {'loop'}, use_global_device_ids=true, to_apply=%region_11.14 | all-reduce | flops 1024 | bytes 8192 | tf_op jit(solution)/shard_map/psum | solution.py:112
  315.9 0.1 copy.34
  316.0 2.9 cholesky.81
  319.0 0.6 compare_reduce_fusion
  319.6 0.7 fusion.42
  320.3 2.4 custom-call.9
  322.7 0.2 convolution_bitcast_fusion
  323.0 0.6 pad_maximum_fusion.3
  323.6 0.7 copy.35
  (26 shorter events, 0.2 us)
Async XLA Ops:
  7.2 31.2 %copy-start = (bf16[1024,32]{0,1:T(8,128)(2,1)S(1)}, bf16[1024,32]{0,1:T(8,128)(2,1)}, u32[]{:S(2)}) copy-start(bf16[1024,32]{0,1:T(8,128)(2,1)} %param.10) | copy-start | bytes 196612
  7.2 31.2 %copy-start.2 = (bf16[256,1024]{1,0:T(8,128)(2,1)S(1)}, bf16[256,1024]{1,0:T(8,128)(2,1)}, u32[]{:S(2)}) copy-start(bf16[256,1024]{1,0:T(8,128)(2,1)} %param.7) | copy-start | bytes 1572868
  7.2 31.0 %copy-start.3 = (s32[8192]{0:T(1024)S(1)}, s32[8192]{0:T(1024)}, u32[]{:S(2)}) copy-start(s32[8192]{0:T(1024)} %param.8) | copy-start | bytes 98308
  7.2 80.9 %copy-start.4 = (s32[256,2]{0,1:T(2,128)S(1)}, s32[256,2]{0,1:T(2,128)}, u32[]{:S(2)}) copy-start(s32[256,2]{0,1:T(2,128)} %param.9) | copy-start | bytes 6148
  7.2 81.4 %all-gather.5.cloned.1.call-start = ((), (), s32[]{:S(2)}) async-start(), calls=%async_computation | async-start | bytes 7864320 | tf_op jit(solution)/shard_map/all_gather | solution.py:54
  7.3 17.1 %collective-permute-start.1 = (bf16[256,1024]{1,0:T(8,128)(2,1)}, bf16[256,1024]{1,0:T(8,128)(2,1)S(1)}, u32[]{:S(2)}, u32[]{:S(2)}) collective-permute-start(bf16[256,1024]{1,0:T(8,128)(2,1)} %param.7), channel_id=1, source_target_pairs={{1,0},{2,1},{3,2},{4,3},{5,4},{6,5},{7,6},{9,8},{10,9},{11,10},{12... | collective-permute-start | bytes 1572872 | tf_op jit(solution)/shard_map/ppermute | solution.py:20
  8.7 27.2 %collective-permute-start = (bf16[256,1024]{1,0:T(8,128)(2,1)}, bf16[256,1024]{1,0:T(8,128)(2,1)S(1)}, u32[]{:S(2)}, u32[]{:S(2)}) collective-permute-start(bf16[256,1024]{1,0:T(8,128)(2,1)} %param.7), channel_id=1, source_target_pairs={{0,1},{1,2},{2,3},{3,4},{4,5},{5,6},{6,7},{8,9},{9,10},{10,11},{11... | collective-permute-start | bytes 1572872 | tf_op jit(solution)/shard_map/ppermute | solution.py:18
  88.7 4.6 %copy-start.1 = (bf16[3072,1024]{1,0:T(8,128)(2,1)S(1)}, bf16[3072,1024]{1,0:T(8,128)(2,1)}, u32[]{:S(2)}) copy-start(bf16[3072,1024]{1,0:T(8,128)(2,1)} %all-gather.5.cloned.1.call-done) | copy-start | bytes 18874372
  100.3 6.1 %collective-permute-start.3 = (f32[256,32]{0,1:T(8,128)S(1)}, f32[256,32]{0,1:T(8,128)S(1)}, u32[]{:S(2)}, u32[]{:S(2)}) collective-permute-start(f32[256,32]{0,1:T(8,128)S(1)} %get-tuple-element.18), channel_id=1, source_target_pairs={{1,0},{2,1},{3,2},{4,3},{5,4},{6,5},{7,6},{9,8},{10,9},{11,10},{12... | collective-permute-start | bytes 98312 | tf_op jit(solution)/shard_map/ppermute | solution.py:20
  101.6 6.4 %collective-permute-start.2 = (f32[256,32]{0,1:T(8,128)S(1)}, f32[256,32]{0,1:T(8,128)S(1)}, u32[]{:S(2)}, u32[]{:S(2)}) collective-permute-start(f32[256,32]{0,1:T(8,128)S(1)} %get-tuple-element.18), channel_id=1, source_target_pairs={{0,1},{1,2},{2,3},{3,4},{4,5},{5,6},{6,7},{8,9},{9,10},{10,11},{11... | collective-permute-start | bytes 98312 | tf_op jit(solution)/shard_map/ppermute | solution.py:18
  213.1 6.7 %collective-permute-start.5 = (f32[256,32]{0,1:T(8,128)S(1)}, f32[256,32]{0,1:T(8,128)S(1)}, u32[]{:S(2)}, u32[]{:S(2)}) collective-permute-start(f32[256,32]{0,1:T(8,128)S(1)} %get-tuple-element.20), channel_id=1, source_target_pairs={{1,0},{2,1},{3,2},{4,3},{5,4},{6,5},{7,6},{9,8},{10,9},{11,10},{12... | collective-permute-start | bytes 98312 | tf_op jit(solution)/shard_map/ppermute | solution.py:20
  214.4 6.1 %collective-permute-start.4 = (f32[256,32]{0,1:T(8,128)S(1)}, f32[256,32]{0,1:T(8,128)S(1)}, u32[]{:S(2)}, u32[]{:S(2)}) collective-permute-start(f32[256,32]{0,1:T(8,128)S(1)} %get-tuple-element.20), channel_id=1, source_target_pairs={{0,1},{1,2},{2,3},{3,4},{4,5},{5,6},{6,7},{8,9},{9,10},{10,11},{11... | collective-permute-start | bytes 98312 | tf_op jit(solution)/shard_map/ppermute | solution.py:18
Sparse Core Ops, SparseCore 0:
  38.3 48.3 all-gather.4
